TPU v7x, 256 devices: a whole 4x4x8 slice. The times are simulated.
256 devices in a mesh: req: 32 (over x, y, core), tp: 8 (over z).
Axes of the slice: x: 4, y: 4, z: 8, core: 2. Of those that a mesh axis runs over, the one named last changes fastest.
Arguments:
- hidden: bfloat16 [8192, 5120], P('req', 'tp'), may hold values from -8 to 8
- q_new: bfloat16 [8192, 5120], P('req', 'tp'), may hold values from -8 to 8
- k_new: bfloat16 [8192, 5120], P('req', 'tp'), may hold values from -8 to 8
- v_new: bfloat16 [8192, 5120], P('req', 'tp'), may hold values from -8 to 8
- cache_k: bfloat16 [32, 4096, 5120], P('req', None, 'tp'), may hold values from -8 to 8
- cache_v: bfloat16 [32, 4096, 5120], P('req', None, 'tp'), may hold values from -8 to 8
- cache_len: int32 [32], replicated, may hold values from 1 to 4096, 32768 in all
- w_out: bfloat16 [5120, 5120], P('tp', 'req'), may hold values from -0.625 to 0.625
- q_cross: bfloat16 [8192, 5120], P('req', 'tp'), may hold values from -8 to 8
- text_k: bfloat16 [4, 512, 5120], P(None, 'req', 'tp'), may hold values from -8 to 8
- text_v: bfloat16 [4, 512, 5120], P(None, 'req', 'tp'), may hold values from -12 to 12
- prompt_of: int32 [32], P('req'), may hold values from 0 to 3, as said below
Outputs:
- hidden_out: bfloat16 [8192, 5120], P('req', 'tp')
- cross_heads: bfloat16 [8192, 5120], P('req', 'tp')
Inputs may be any that keep to these rules, and one draw needn't show every extreme that they name: `cache_len`: cache rows at or beyond a request's length hold no data; the longest request fills all 4096 rows. `prompt_of`: each of the 4 prompts serves exactly 8 requests.
All inputs are finite; a program needn't handle non-finite values.
Results may differ from a plain program's by a relative error of at most 0.014.
Values may be sent and summed in bfloat16 or wider, within the bound.
A program may use at most 128 MiB of HBM per device.

v0:
```python
import jax
import jax.numpy as jnp
from jax import lax
from jax.sharding import PartitionSpec as P

HD = 128
BLOCK = 512


NEG_FILL = -1e30


def attend(running, queries, key_block, value_block, visible, score_scale):
    totals, maxima, masses = running
    scores = (
        jnp.einsum("qhd,khd->hqk", queries, key_block, preferred_element_type=jnp.float32)
        * score_scale
    )
    scores = jnp.where(visible[None], scores, NEG_FILL)
    top_new = jnp.maximum(maxima, jnp.max(scores, axis=-1))
    weights = jnp.where(visible[None], jnp.exp(scores - top_new[..., None]), 0.0)
    shrink = jnp.exp(maxima - top_new)
    masses = masses * shrink + jnp.sum(weights, axis=-1)
    totals = totals * shrink[..., None] + jnp.einsum(
        "hqk,khd->hqd",
        weights.astype(jnp.bfloat16),
        value_block,
        preferred_element_type=jnp.float32,
    )
    return (totals, top_new, masses)


def cache_pass(
    running, queries, key_rows, value_rows, block_count, row_limit, block_rows, score_scale
):
    query_rows = queries.shape[0]

    def visit_block(block_index, carried):
        first_row = block_index * block_rows
        key_block = lax.dynamic_slice_in_dim(key_rows, first_row, block_rows, 0)
        value_block = lax.dynamic_slice_in_dim(value_rows, first_row, block_rows, 0)
        live_rows = first_row + jnp.arange(block_rows, dtype=jnp.int32) < row_limit
        visible = jnp.broadcast_to(live_rows[None, :], (query_rows, block_rows))
        return attend(carried, queries, key_block, value_block, visible, score_scale)

    return lax.fori_loop(0, block_count, visit_block, running)


def finish_heads(running):
    totals, maxima, masses = running
    output = totals / masses[..., None]
    return (
        output.transpose(1, 0, 2)
        .reshape(totals.shape[1], totals.shape[0] * totals.shape[2])
        .astype(jnp.bfloat16)
    )


def per_device(
    hidden,
    q_new,
    k_new,
    v_new,
    cache_k,
    cache_v,
    cache_len,
    w_out,
    q_cross,
    text_k,
    text_v,
    prompt_of,
):
    row_count, width_local = q_new.shape
    head_count = width_local // HD
    capacity = cache_k.shape[1]
    score_scale = HD ** (-0.5)
    block_rows = BLOCK
    queries = q_new.reshape(row_count, head_count, HD)
    new_keys = k_new.reshape(row_count, head_count, HD)
    new_values = v_new.reshape(row_count, head_count, HD)
    cached_keys = cache_k[0].reshape(capacity, head_count, HD)
    cached_values = cache_v[0].reshape(capacity, head_count, HD)
    req_place = lax.axis_index("req")
    length = lax.dynamic_index_in_dim(cache_len, req_place, 0, keepdims=False)
    empty_state = (
        jnp.zeros((head_count, row_count, HD), jnp.float32),
        jnp.full((head_count, row_count), NEG_FILL, jnp.float32),
        jnp.zeros((head_count, row_count), jnp.float32),
    )
    blocks_live = (length + block_rows - 1) // block_rows
    running = cache_pass(
        empty_state,
        queries,
        cached_keys,
        cached_values,
        blocks_live,
        length,
        block_rows,
        score_scale,
    )
    row_ids = jnp.arange(row_count, dtype=jnp.int32)
    causal = row_ids[:, None] >= row_ids[None, :]
    running = attend(running, queries, new_keys, new_values, causal, score_scale)
    self_heads = finish_heads(running)
    terms = jnp.dot(
        self_heads,
        lax.all_gather(w_out, "req", axis=1, tiled=True),
        preferred_element_type=jnp.float32,
    )
    summed = lax.psum_scatter(
        terms.astype(jnp.bfloat16), "tp", scatter_dimension=1, tiled=True
    ).astype(jnp.float32)
    hidden_out = (hidden.astype(jnp.float32) + summed).astype(jnp.bfloat16)
    prompt = prompt_of[0]
    cross_queries = q_cross.reshape(row_count, head_count, HD)
    text_keys = lax.dynamic_index_in_dim(
        lax.all_gather(text_k, "req", axis=1, tiled=True), prompt, 0, keepdims=False
    )
    text_values = lax.dynamic_index_in_dim(
        lax.all_gather(text_v, "req", axis=1, tiled=True), prompt, 0, keepdims=False
    )
    piece_rows = text_keys.shape[0]
    text_keys = text_keys.reshape(piece_rows, head_count, HD)
    text_values = text_values.reshape(piece_rows, head_count, HD)
    visible = jnp.ones((row_count, piece_rows), dtype=bool)
    crossed = attend(empty_state, cross_queries, text_keys, text_values, visible, score_scale)
    cross_heads = finish_heads(crossed)
    return (hidden_out, cross_heads)


def solution(mesh):
    placed = (
        P("req", "tp"),
        P("req", "tp"),
        P("req", "tp"),
        P("req", "tp"),
        P("req", None, "tp"),
        P("req", None, "tp"),
        P(),
        P("tp", "req"),
        P("req", "tp"),
        P(None, "req", "tp"),
        P(None, "req", "tp"),
        P("req"),
    )
    return jax.shard_map(
        per_device,
        mesh=mesh,
        in_specs=placed,
        out_specs=(P("req", "tp"), P("req", "tp")),
        check_vma=False,
    )
```

profile of v0, /device:TPU:2, one launch (start us, length us, event | category | flops | bytes accessed | tf_op | source)
XLA Modules:
  0.0 225.6 jit_solution(18249106534673599268)
XLA Ops:
  7.2 0.7 all-gather.4.cloned.1.call-update
  7.9 1.6 copy.56
  9.6 0.7 all-gather.8.cloned.1.call-update
  10.3 1.3 dynamic_slice.17
  12.2 1.1 copy.45
  13.6 7.9 %copy.44 = bf16[1,4096,640]{1,2,0:T(8,128)(2,1)} copy(bf16[1,4096,640]{2,1,0:T(8,128)(2,1)} %param.18) | data formatting | bytes 10485760 | tf_op args[4]
  21.5 8.0 %copy.46 = bf16[1,4096,640]{1,2,0:T(8,128)(2,1)} copy(bf16[1,4096,640]{2,1,0:T(8,128)(2,1)} %param.19) | data formatting | bytes 10485760 | tf_op args[5]
  29.8 34.2 %while.14 = (s32[]{:T(128)}, f32[5,256,128]{2,1,0:T(8,128)S(1)}, f32[5,256]{1,0:T(8,128)S(1)}, f32[5,256]{1,0:T(8,128)S(1)}, s32[]{:T(128)}, /*index=5*/s32[]{:T...) while((s32[]{:T(128)}, f32[5,256,128]{2,1,0:T(8,128)S(1)}, ...), condition=%wide.region_3.4_spmd, body=%wide.region_0.3_spmd.sunk | while | flops 344395264 | bytes 10904251 | solution.py:46
  29.8 0.7 add_compare_fusion.2
  30.5 1.8 bitcast_reduce_fusion.3
  32.3 0.7 fusion.67
  33.0 2.4 %fusion.68 = f32[5,256,128]{2,1,0:T(8,128)S(1)} fusion(f32[5,512,256]{2,1,0:T(8,128)S(1)} %get-tuple-element.169, f32[5,256]{1,0:T(8,128)S(1)} %max.8, pred[512]{0:T(512)(128)(4,1)S(1)} %add_compare_fusion.2, bf16[4096,5,128]{0,2,1:T(8,128)(2,1)} %get-tuple-element.207, s32[]{:T(128)S(6)} %select_n.81, f32[5,256,128]{2,1,0:T(8,128)S(1)} %get-tuple-element.187, ...), kind=kOutput, calls=%fused_computation.10.clone.1 | convolution fusion | flops 171376640 | bytes 4604932 | tf_op jit(solution)/shard_map/while/body/hqk,khd->hqd/dot_general | solution.py:24
  35.5 0.6 add_compare_fusion.2
  36.1 1.8 bitcast_reduce_fusion.3
  37.9 0.7 fusion.67
  38.7 2.4 %fusion.68 = f32[5,256,128]{2,1,0:T(8,128)S(1)} fusion(f32[5,512,256]{2,1,0:T(8,128)S(1)} %get-tuple-element.169, f32[5,256]{1,0:T(8,128)S(1)} %max.8, pred[512]{0:T(512)(128)(4,1)S(1)} %add_compare_fusion.2, bf16[4096,5,128]{0,2,1:T(8,128)(2,1)} %get-tuple-element.207, s32[]{:T(128)S(6)} %select_n.81, f32[5,256,128]{2,1,0:T(8,128)S(1)} %get-tuple-element.187, ...), kind=kOutput, calls=%fused_computation.10.clone.1 | convolution fusion | flops 171376640 | bytes 4604932 | tf_op jit(solution)/shard_map/while/body/hqk,khd->hqd/dot_general | solution.py:24
  41.2 0.6 add_compare_fusion.2
  41.8 1.8 bitcast_reduce_fusion.3
  43.6 0.7 fusion.67
  44.3 2.4 %fusion.68 = f32[5,256,128]{2,1,0:T(8,128)S(1)} fusion(f32[5,512,256]{2,1,0:T(8,128)S(1)} %get-tuple-element.169, f32[5,256]{1,0:T(8,128)S(1)} %max.8, pred[512]{0:T(512)(128)(4,1)S(1)} %add_compare_fusion.2, bf16[4096,5,128]{0,2,1:T(8,128)(2,1)} %get-tuple-element.207, s32[]{:T(128)S(6)} %select_n.81, f32[5,256,128]{2,1,0:T(8,128)S(1)} %get-tuple-element.187, ...), kind=kOutput, calls=%fused_computation.10.clone.1 | convolution fusion | flops 171376640 | bytes 4604932 | tf_op jit(solution)/shard_map/while/body/hqk,khd->hqd/dot_general | solution.py:24
  46.8 0.6 add_compare_fusion.2
  47.5 1.8 bitcast_reduce_fusion.3
  49.2 0.7 fusion.67
  50.0 2.4 %fusion.68 = f32[5,256,128]{2,1,0:T(8,128)S(1)} fusion(f32[5,512,256]{2,1,0:T(8,128)S(1)} %get-tuple-element.169, f32[5,256]{1,0:T(8,128)S(1)} %max.8, pred[512]{0:T(512)(128)(4,1)S(1)} %add_compare_fusion.2, bf16[4096,5,128]{0,2,1:T(8,128)(2,1)} %get-tuple-element.207, s32[]{:T(128)S(6)} %select_n.81, f32[5,256,128]{2,1,0:T(8,128)S(1)} %get-tuple-element.187, ...), kind=kOutput, calls=%fused_computation.10.clone.1 | convolution fusion | flops 171376640 | bytes 4604932 | tf_op jit(solution)/shard_map/while/body/hqk,khd->hqd/dot_general | solution.py:24
  52.5 0.6 add_compare_fusion.2
  53.1 1.8 bitcast_reduce_fusion.3
  54.9 0.7 fusion.67
  55.7 2.4 %fusion.68 = f32[5,256,128]{2,1,0:T(8,128)S(1)} fusion(f32[5,512,256]{2,1,0:T(8,128)S(1)} %get-tuple-element.169, f32[5,256]{1,0:T(8,128)S(1)} %max.8, pred[512]{0:T(512)(128)(4,1)S(1)} %add_compare_fusion.2, bf16[4096,5,128]{0,2,1:T(8,128)(2,1)} %get-tuple-element.207, s32[]{:T(128)S(6)} %select_n.81, f32[5,256,128]{2,1,0:T(8,128)S(1)} %get-tuple-element.187, ...), kind=kOutput, calls=%fused_computation.10.clone.1 | convolution fusion | flops 171376640 | bytes 4604932 | tf_op jit(solution)/shard_map/while/body/hqk,khd->hqd/dot_general | solution.py:24
  58.2 0.6 add_compare_fusion.2
  58.8 1.8 bitcast_reduce_fusion.3
  60.6 0.7 fusion.67
  61.3 2.4 %fusion.68 = f32[5,256,128]{2,1,0:T(8,128)S(1)} fusion(f32[5,512,256]{2,1,0:T(8,128)S(1)} %get-tuple-element.169, f32[5,256]{1,0:T(8,128)S(1)} %max.8, pred[512]{0:T(512)(128)(4,1)S(1)} %add_compare_fusion.2, bf16[4096,5,128]{0,2,1:T(8,128)(2,1)} %get-tuple-element.207, s32[]{:T(128)S(6)} %select_n.81, f32[5,256,128]{2,1,0:T(8,128)S(1)} %get-tuple-element.187, ...), kind=kOutput, calls=%fused_computation.10.clone.1 | convolution fusion | flops 171376640 | bytes 4604932 | tf_op jit(solution)/shard_map/while/body/hqk,khd->hqd/dot_general | solution.py:24
  64.5 0.4 fusion.49
  65.5 1.4 all-gather.4.cloned.1.call-done
  67.0 5.1 %convolution_convert_fusion = bf16[256,5120]{1,0:T(8,128)(2,1)S(1)} fusion(bf16[256,640]{0,1:T(8,128)(2,1)S(1)} %bitcast.94, bf16[640,5120]{0,1:T(8,128)(2,1)} %all-gather.4.cloned.1.call-done), kind=kOutput, calls=%fused_computation.22 | convolution fusion | flops 1679032320 | bytes 9502720 | tf_op jit(solution)/shard_map/dot_general | solution.py:105
  72.1 2.6 %copy.71 = bf16[256,5120]{0,1:T(8,128)(2,1)} copy(bf16[256,5120]{1,0:T(8,128)(2,1)S(1)} %convolution_convert_fusion) | data formatting | bytes 5242880
  75.8 43.1 %all-gather.6.cloned.1.call-done = bf16[4,512,640]{2,0,1:T(4,128)(2,1)} async-done(((bf16[4,16,640]{2,0,1:T(4,128)(2,1)}), bf16[4,512,640]{2,0,1:T(4,128)(2,1)}) %all-gather.6.cloned.1.call-update) | async-done | bytes 2621456 | tf_op jit(solution)/shard_map/all_gather | solution.py:117
  119.0 3.1 %constant_dynamic-slice_fusion.1 = bf16[1,512,640]{2,0,1:T(2,128)(2,1)S(1)} fusion(bf16[4,512,640]{2,0,1:T(4,128)(2,1)} %all-gather.6.cloned.1.call-done, s32[]{:T(128)S(6)} %select_n.42), kind=kLoop, calls=%fused_computation.54 | loop fusion | bytes 1310724 | tf_op jit(solution)/shard_map/jit(dynamic_index_in_dim)/dynamic_slice | solution.py:116
  122.1 1.0 copy.75
  123.0 47.3 %all-gather.8.cloned.1.call-done = bf16[4,512,640]{2,1,0:T(8,128)(2,1)} async-done(((bf16[4,16,640]{2,1,0:T(8,128)(2,1)}), bf16[4,512,640]{2,1,0:T(8,128)(2,1)}) %all-gather.8.cloned.1.call-update) | async-done | bytes 2621456 | tf_op jit(solution)/shard_map/all_gather | solution.py:120
  170.3 1.1 constant_dynamic-slice_fusion
  171.7 0.6 bitcast_reduce_fusion.1
  172.3 0.4 fusion.20
  172.8 0.7 fusion.37
  173.4 0.9 copy.63
  174.3 42.7 %reduce-scatter.4.cloned.1.call-done = bf16[640,256]{1,0:T(8,128)(2,1)} async-done(((bf16[5120,256]{1,0:T(8,128)(2,1)}), bf16[640,256]{1,0:T(8,128)(2,1)}) %reduce-scatter.4.cloned.1.call-update) | async-done | bytes 327696
  217.1 1.2 copy.72
  218.3 0.8 add_convert_fusion
  (48 shorter events, 2.5 us)
Async XLA Ops:
  7.2 59.8 %all-gather.4.cloned.1.call-start = ((), (), s32[]{:S(2)}) async-start(), calls=%async_computation.1 | async-start | bytes 6758400 | tf_op jit(solution)/shard_map/all_gather | solution.py:107
  7.9 111.1 %all-gather.6.cloned.1.call-start = ((), (), s32[]{:S(2)}) async-start(), calls=%async_computation.2 | async-start | bytes 2703360 | tf_op jit(solution)/shard_map/all_gather | solution.py:117
  9.5 160.8 %all-gather.8.cloned.1.call-start = ((), (), s32[]{:S(2)}) async-start(), calls=%async_computation.3 | async-start | bytes 2703360 | tf_op jit(solution)/shard_map/all_gather | solution.py:120
  10.3 206.8 %reduce-scatter.4.cloned.1.call-start = ((), (), s32[]{:S(2)}) async-start(), calls=%async_computation.4 | async-start | bytes 2949120
  21.5 8.0 %copy-start = (bf16[256,640]{1,0:T(8,128)(2,1)S(1)}, bf16[256,640]{1,0:T(8,128)(2,1)}, u32[]{:S(2)}) copy-start(bf16[256,640]{1,0:T(8,128)(2,1)} %param.16) | copy-start | bytes 983044
  29.8 34.5 %copy-start.1 = (bf16[256,640]{1,0:T(8,128)(2,1)S(1)}, bf16[256,640]{1,0:T(8,128)(2,1)}, u32[]{:S(2)}) copy-start(bf16[256,640]{1,0:T(8,128)(2,1)} %param.17) | copy-start | bytes 983044
  74.7 1.0 copy-start.2
  172.8 45.5 %copy-start.3 = (bf16[256,640]{1,0:T(8,128)(2,1)S(1)}, bf16[256,640]{1,0:T(8,128)(2,1)}, u32[]{:S(2)}) copy-start(bf16[256,640]{1,0:T(8,128)(2,1)} %param.14) | copy-start | bytes 983044
Sparse Core Ops, SparseCore 0:
  10.5 56.4 all-gather.3
  70.1 48.8 all-gather.5
  121.6 48.6 all-gather.7
  172.7 44.3 reduce-scatter.3
where the time goes:
time: 227 us; the launch traced here: 226 us
  waiting for transfers between devices  136 us (60%)
  matrix products  32.4 us (14%)
  local copies, waits for them, and re-layouts  31.3 us (14%)
  between operations  15.3 us (7%)
  other arithmetic  9.87 us (4%)
    all_gather x1, waiting for transfers between devices, per_device(): lax.all_gather(text_v, 'req', axis=1, tiled=True)  47.3 us
    unnamed x5, waiting for transfers between devices  44.1 us
    all_gather x1, waiting for transfers between devices, per_device(): lax.all_gather(text_k, 'req', axis=1, tiled=True)  43.1 us
    unnamed x19, local copies, waits for them, and re-layouts  25 us
    dot_general x8, matrix products, attend(): jnp.einsum('hqk,khd->hqd', weights.astype(jnp.bfloat16), value_block, pre...  15.7 us
    dot_general x8, matrix products, attend(): jnp.einsum('qhd,khd->hqk', queries, key_block, preferred_element_type=jnp...  11.6 us
    dot_general x1, matrix products, per_device(): jnp.dot(self_heads, lax.all_gather(w_out, 'req', axis=1, tiled=True), pre...  5.11 us
    reduce_sum x8, other arithmetic, attend(): masses = masses * shrink + jnp.sum(weights, axis=-1)  5.09 us
  transfers between devices with their start and end apart: 4, of which 4 were waited for; matrix products, arithmetic and copies ran while one was open for 32% of the time, Pallas kernels for 0%

commit v1 on v0

v1 whole, which is shorter than its diff:
```python
import jax
import jax.numpy as jnp
from jax import lax
from jax.experimental import pallas as pl
from jax.experimental.pallas import tpu as pltpu
from jax.sharding import PartitionSpec as P

MESH = pl.DeviceIdType.MESH
HD = 128
NH = 5
ROWS = 256
W = NH * HD
CAP = 4096
KEYS = CAP + ROWS
CHUNK = 512
NEG = -1e30
SCALE = HD**-0.5
LOG2E = 1.4426950408889634
NT = (((1,), (1,)), ((), ()))
F32 = jnp.float32
BF16 = jnp.bfloat16


def kernel(
    len_ref, prompt_ref, hid_h, q_h, kn_h, vn_h, ck_h, cv_h, w_h, qc_h, tk_h, tv_h,
    out_h, cross_h,
    q_s, kn_s, vn_s, hid_s, qc_s, k_s, v_s, wloc, wall, tk, tv, sbuf, bias, caus,
    mrun, mfin, lrun, acc, heads, rs_in, rs_out, outb, crossb,
    lsem, kvsem, grecv, gsib, gsend, rrecv, rsend,
):
    me = lax.axis_index("req")
    z = lax.axis_index("tp")
    x, y, c = me // 8, (me // 2) % 4, me % 2
    d = 1 - 2 * c

    def rid(ax, ay, ac):
        return (((ax + 8) % 4) * 4 + (ay + 8) % 4) * 2 + ac

    sib = (rid(x, y, 1 - c), z)
    zp = (me, (z + 1) % 8)
    zm = (me, (z + 7) % 8)

    def shift(axis, by):
        if axis == "x":
            return (rid(x + by, y, c), z)
        return (rid(x, y + by, c), z)

    wcopy = pltpu.make_async_copy(w_h, wloc, lsem.at[0])
    wcopy.start()
    small = [
        pltpu.make_async_copy(src, dst, lsem.at[i])
        for i, (src, dst) in enumerate([(q_h, q_s), (kn_h, kn_s), (vn_h, vn_s), (hid_h, hid_s), (qc_h, qc_s)], 1)
    ]
    for cp in small[:3]:
        cp.start()

    def kv_copy(h):
        return (
            pltpu.make_async_copy(ck_h.at[0, :, pl.ds(h * HD, HD)], k_s.at[h], kvsem.at[0, h]),
            pltpu.make_async_copy(cv_h.at[0, :, pl.ds(h * HD, HD)], v_s.at[h], kvsem.at[1, h]),
        )

    kv = [kv_copy(h) for h in range(NH)]
    for kc, vc in kv:
        kc.start()
        vc.start()
    own_text = (
        pltpu.make_async_copy(tk_h, tk.at[me], lsem.at[6]),
        pltpu.make_async_copy(tv_h, tv.at[me], lsem.at[7]),
    )
    for cp in own_text:
        cp.start()
    for cp in small[3:]:
        cp.start()

    barrier = pltpu.get_barrier_semaphore()
    nbrs = (shift("x", 1), shift("x", -1), shift("y", 1), shift("y", -1), sib, zp, zm)
    for nb in nbrs:
        pl.semaphore_signal(barrier, inc=1, device_id=nb, device_id_type=MESH)

    wcopy.wait()
    mine = pl.multiple_of(me * 160, 32)
    wall[pl.ds(mine, 128), :] = wloc[:, 0:128].T
    wall[pl.ds(pl.multiple_of(mine + 128, 32), 32), :] = wloc[:, 128:160].T

    length = len_ref[me]
    col = lax.broadcasted_iota(jnp.int32, (8, CAP), 1)
    bias[...] = jnp.where(col < length, 0.0, NEG).astype(F32)
    ri = lax.broadcasted_iota(jnp.int32, (ROWS, ROWS), 0)
    ci = lax.broadcasted_iota(jnp.int32, (ROWS, ROWS), 1)
    caus[...] = jnp.where(ci <= ri, 0.0, NEG).astype(F32)

    def piece(p, ab, ax, ay, ac):
        r = rid(ax, ay, ac)
        if p == 0:
            return wall.at[pl.ds(pl.multiple_of(r * 160 + ab * 80, 16), 80)]
        return (tk if ab == 0 else tv).at[r]

    def some(p, ab, n):
        if p == 0:
            return wall.at[pl.ds(0, 80 * n)]
        return (tk if ab == 0 else tv).at[pl.ds(0, n)]

    class Gather:
        def __init__(self, p, ab):
            self.p, self.ab = p, ab
            self.f, self.g = ("y", "x") if ab == 0 else ("x", "y")

        def ref(self, rf, rg):
            if self.ab == 0:
                return piece(self.p, self.ab, x + rg, y + rf, c)
            return piece(self.p, self.ab, x + rf, y + rg, c)

        def copy(self, ref, dev, rf, rg):
            return pltpu.make_async_remote_copy(
                src_ref=ref, dst_ref=ref,
                send_sem=gsend.at[self.p, self.ab],
                recv_sem=grecv.at[self.p, self.ab, (rf % 4) * 4 + rg % 4],
                device_id=dev, device_id_type=MESH,
            )

        def to_f(self, rf, rg, by, nf):
            self.copy(self.ref(rf, rg), shift(self.f, by), nf, 0).start()

        def to_g(self, rf, rg, by, nf, ng):
            self.copy(self.ref(rf, rg), shift(self.g, by), nf, ng).start()

        def both_g(self, rf):
            for by in (1, -1):
                self.to_g(rf, 0, by, rf, -by)

        def to_sib(self, rf, rg):
            ref = self.ref(rf, rg)
            pltpu.make_async_remote_copy(
                src_ref=ref, dst_ref=ref,
                send_sem=gsend.at[self.p, self.ab],
                recv_sem=gsib.at[self.p, self.ab],
                device_id=sib, device_id_type=MESH,
            ).start()

        def wait(self, rf, rg):
            self.copy(self.ref(rf, rg), sib, rf, rg).wait_recv()

        def wait_sib(self):
            ref = some(self.p, self.ab, 16)
            pltpu.make_async_remote_copy(
                src_ref=ref, dst_ref=ref,
                send_sem=gsend.at[self.p, self.ab],
                recv_sem=gsib.at[self.p, self.ab],
                device_id=sib, device_id_type=MESH,
            ).wait_recv()

        def wait_send(self):
            self.copy(some(self.p, self.ab, 31), sib, 0, 0).wait_send()

    pairs = [(Gather(0, 0), Gather(0, 1)), (Gather(1, 0), Gather(1, 1))]

    def stage(p, n):
        gs = pairs[p]
        if n == 0:
            for g in gs:
                for by in (1, -1):
                    g.to_f(0, 0, by, -by)
            for g in gs:
                g.both_g(0)
            for g in gs:
                g.to_sib(0, 0)
        elif n == 1:
            for g in gs:
                g.wait(1, 0)
                g.wait(3, 0)
                g.to_f(-d, 0, d, 2)
                g.both_g(1)
                g.both_g(3)
            for g in gs:
                g.to_sib(1, 0)
                g.to_sib(3, 0)
        elif n == 2:
            for g in gs:
                g.wait(2, 0)
                g.both_g(2)
            for g in gs:
                g.wait(0, 1)
                g.wait(0, 3)
                g.to_g(0, -d, d, 0, 2)
            for g in gs:
                g.to_sib(2, 0)
                g.to_sib(0, 1)
                g.to_sib(0, 3)
        elif n == 3:
            for g in gs:
                for rf in (1, 3):
                    g.wait(rf, 1)
                    g.wait(rf, 3)
                    g.to_g(rf, -d, d, rf, 2)
            for g in gs:
                for rf in (1, 3):
                    g.to_sib(rf, 1)
                    g.to_sib(rf, 3)
        elif n == 4:
            for g in gs:
                g.wait(2, 1)
                g.wait(2, 3)
                g.to_g(2, -d, d, 2, 2)
                g.wait(0, 2)
            for g in gs:
                g.to_sib(2, 1)
                g.to_sib(2, 3)
                g.to_sib(0, 2)
        elif n == 5:
            for g in gs:
                for rf in (1, 3):
                    g.wait(rf, 2)
                    g.to_sib(rf, 2)
        elif n == 6:
            for g in gs:
                g.wait(2, 2)
                g.to_sib(2, 2)
        else:
            for g in gs:
                g.wait_sib()

    def qk_new(h):
        sl = slice(h * HD, (h + 1) * HD)
        s = lax.dot_general(q_s[:, sl], kn_s[:, sl], NT, preferred_element_type=F32)
        s = s + caus[...]
        sbuf[h % 2, :, CAP:KEYS] = s
        mrun[...] = jnp.maximum(s[:, 0:128], s[:, 128:256])

    def qk_chunk(h, i):
        sl = slice(h * HD, (h + 1) * HD)
        at = pl.multiple_of(i * CHUNK, CHUNK)
        s = lax.dot_general(q_s[:, sl], k_s[h, pl.ds(at, CHUNK), :], NT, preferred_element_type=F32)
        s = s + bias[0:1, pl.ds(at, CHUNK)]
        sbuf[h % 2, :, pl.ds(at, CHUNK)] = s
        m = jnp.maximum(jnp.maximum(s[:, 0:128], s[:, 128:256]), jnp.maximum(s[:, 256:384], s[:, 384:512]))
        mrun[...] = jnp.maximum(mrun[...], m)

    def set_max():
        mfin[...] = jnp.broadcast_to(jnp.max(mrun[...], axis=1, keepdims=True), (ROWS, HD))

    def pv(p, v, lane_tiles):
        part = p[:, 0:128]
        for t in range(1, lane_tiles):
            part = part + p[:, t * 128:(t + 1) * 128]
        return part, jnp.dot(p.astype(BF16), v, preferred_element_type=F32)

    def weigh(s, lane_tiles):
        m = mfin[...]
        return jnp.concatenate(
            [jnp.exp2((s[:, t * 128:(t + 1) * 128] - m) * (SCALE * LOG2E)) for t in range(lane_tiles)], axis=1
        )

    def pv_new(h):
        sl = slice(h * HD, (h + 1) * HD)
        p = weigh(sbuf[h % 2, :, CAP:KEYS], 2)
        part, o = pv(p, vn_s[:, sl], 2)
        lrun[...] = part
        acc[...] = o

    def pv_chunk(h, i):
        at = pl.multiple_of(i * CHUNK, CHUNK)
        p = weigh(sbuf[h % 2, :, pl.ds(at, CHUNK)], 4)
        part, o = pv(p, v_s[h, pl.ds(at, CHUNK), :], 4)
        lrun[...] += part
        acc[...] += o

    def head_stage(h):
        if h < NH:
            kv[h][0].wait()
        if h > 0:
            kv[h - 1][1].wait()
            pv_new(h - 1)
        if h < NH:
            qk_new(h)

        @pl.loop(0, CAP // CHUNK)
        def _(i):
            if h < NH:
                qk_chunk(h, i)
            if h > 0:
                pv_chunk(h - 1, i)

        if h > 0:
            mass = jnp.sum(lrun[...], axis=1, keepdims=True)
            heads[:, (h - 1) * HD:h * HD] = (acc[...] / mass).astype(BF16)
        if h < NH:
            set_max()

    prompt = prompt_ref[0]

    def cross_head(h):
        sl = slice(h * HD, (h + 1) * HD)
        kt = tk[:, prompt, :, sl].reshape(512, HD)
        vt = tv[:, prompt, :, sl].reshape(512, HD)
        s = lax.dot_general(qc_s[:, sl], kt, NT, preferred_element_type=F32)
        m = jnp.max(s, axis=1, keepdims=True)
        p = jnp.exp2((s - m) * (SCALE * LOG2E))
        mass = jnp.sum(p, axis=1, keepdims=True)
        o = jnp.dot(p.astype(BF16), vt, preferred_element_type=F32)
        crossb[:, sl] = (o / mass).astype(BF16)

    groups = ((0, 3), (3, 2))

    def term(g, s):
        first, count = groups[g]
        way = d if g == 0 else -d
        b = (z - way * (1 + s) + 16) % 8
        at = pl.multiple_of(b * W + first * HD, HD)
        wt = wall[pl.ds(at, count * HD), :]
        return lax.dot_general(heads[...], wt, NT, preferred_element_type=F32)

    def rs_copy(g, j, s):
        way = d if g == 0 else -d
        return pltpu.make_async_remote_copy(
            src_ref=rs_out.at[j, s], dst_ref=rs_in.at[j, s],
            send_sem=rsend.at[j, s], recv_sem=rrecv.at[j, s],
            device_id=(me, (z + way + 8) % 8), device_id_type=MESH,
        )

    def rs_first():
        for g, (first, count) in enumerate(groups):
            t = term(g, 0)
            for k in range(count):
                rs_out[first + k, 0] = t[:, k * HD:(k + 1) * HD].astype(BF16)
            for k in range(count):
                rs_copy(g, first + k, 0).start()

    def rs_step(s):
        for g, (first, count) in enumerate(groups):
            t = term(g, s + 1)
            for k in range(count):
                j = first + k
                rs_copy(g, j, s).wait_recv()
                total = rs_in[j, s].astype(F32) + t[:, k * HD:(k + 1) * HD]
                if s < 6:
                    rs_out[j, s + 1] = total.astype(BF16)
                    rs_copy(g, j, s + 1).start()
                else:
                    sl = slice(j * HD, (j + 1) * HD)
                    outb[:, sl] = (hid_s[:, sl].astype(F32) + total).astype(BF16)

    pl.semaphore_wait(barrier, len(nbrs))
    stage(0, 0)
    for cp in small[:3]:
        cp.wait()
    head_stage(0)
    head_stage(1)
    stage(0, 1)
    head_stage(2)
    head_stage(3)
    stage(0, 2)
    head_stage(4)
    stage(0, 3)
    head_stage(5)
    for cp in own_text:
        cp.wait()
    stage(0, 4)
    stage(1, 0)
    stage(0, 5)
    stage(0, 6)
    stage(0, 7)
    rs_first()
    for cp in small[3:]:
        cp.wait()
    rs_step(0)
    stage(1, 1)
    rs_step(1)
    stage(1, 2)
    rs_step(2)
    stage(1, 3)
    rs_step(3)
    stage(1, 4)
    rs_step(4)
    stage(1, 5)
    stage(1, 6)
    stage(1, 7)
    cross_head(0)
    cross_head(1)
    cross_head(2)
    rs_step(5)
    cross_head(3)
    cross_head(4)
    cross_out = pltpu.make_async_copy(crossb, cross_h, lsem.at[8])
    cross_out.start()
    rs_step(6)
    hid_out = pltpu.make_async_copy(outb, out_h, lsem.at[9])
    hid_out.start()
    for ps in pairs:
        for g in ps:
            g.wait_send()
    for g, (first, count) in enumerate(groups):
        for k in range(count):
            for s in range(7):
                rs_copy(g, first + k, s).wait_send()
    cross_out.wait()
    hid_out.wait()


def per_device(
    hidden, q_new, k_new, v_new, cache_k, cache_v, cache_len, w_out, q_cross, text_k, text_v, prompt_of,
):
    any_spec = pl.BlockSpec(memory_space=pl.ANY)
    smem = pl.BlockSpec(memory_space=pltpu.SMEM)
    v = pltpu.VMEM
    dma = pltpu.SemaphoreType.DMA
    return pl.pallas_call(
        kernel,
        out_shape=(
            jax.ShapeDtypeStruct((ROWS, W), BF16),
            jax.ShapeDtypeStruct((ROWS, W), BF16),
        ),
        in_specs=[smem, smem] + [any_spec] * 10,
        out_specs=(any_spec, any_spec),
        scratch_shapes=[
            v((ROWS, W), BF16), v((ROWS, W), BF16), v((ROWS, W), BF16), v((ROWS, W), BF16), v((ROWS, W), BF16),
            v((NH, CAP, HD), BF16), v((NH, CAP, HD), BF16),
            v((W, 160), BF16), v((8 * W, W), BF16),
            v((32, 4, 16, W), BF16), v((32, 4, 16, W), BF16),
            v((2, ROWS, KEYS), F32), v((8, CAP), F32), v((ROWS, ROWS), F32),
            v((ROWS, HD), F32), v((ROWS, HD), F32), v((ROWS, HD), F32), v((ROWS, HD), F32),
            v((ROWS, W), BF16),
            v((NH, 7, ROWS, HD), BF16), v((NH, 7, ROWS, HD), BF16),
            v((ROWS, W), BF16), v((ROWS, W), BF16),
            dma((10,)), dma((2, NH)), dma((2, 2, 16)), dma((2, 2)), dma((2, 2)), dma((NH, 7)), dma((NH, 7)),
        ],
        compiler_params=pltpu.CompilerParams(
            collective_id=0, has_side_effects=True, vmem_limit_bytes=60 * 1024 * 1024
        ),
    )(cache_len, prompt_of, hidden, q_new, k_new, v_new, cache_k, cache_v, w_out, q_cross, text_k, text_v)


def solution(mesh):
    placed = (
        P("req", "tp"), P("req", "tp"), P("req", "tp"), P("req", "tp"),
        P("req", None, "tp"), P("req", None, "tp"),
        P(), P("tp", "req"), P("req", "tp"),
        P(None, "req", "tp"), P(None, "req", "tp"), P("req"),
    )
    return jax.shard_map(
        per_device,
        mesh=mesh,
        in_specs=placed,
        out_specs=(P("req", "tp"), P("req", "tp")),
        check_vma=False,
    )
```

time: 227 us -> 78 us (0.34)
  the two profiles are of different devices: /device:TPU:2 before, /device:TPU:1 now
where the time goes in v1:
time: 78 us; the launch traced here: 77.8 us
  Pallas kernels  71.2 us (91%)
  local copies, waits for them, and re-layouts  5.28 us (7%)
  between operations  1.29 us (2%)
    pallas_call x1, Pallas kernels, per_device(): pl.pallas_call(kernel, out_shape=(jax.ShapeDtypeStruct((ROWS, W), BF16),...  71.2 us
    unnamed x3, local copies, waits for them, and re-layouts  5.28 us

profile of v1, /device:TPU:1, one launch (start us, length us, event | category | flops | bytes accessed | tf_op | source)
XLA Modules:
  0.0 77.8 jit_solution(11513252799102556370)
XLA Ops:
  1.3 1.8 %copy.14.w_h = bf16[640,160]{1,0:T(8,128)(2,1)} copy(bf16[640,160]{0,1:T(8,128)(2,1)} %param.19) | data formatting | bytes 409600 | tf_op args[7]
  3.1 71.2 %shard_map.131 = (bf16[256,640]{1,0:T(8,128)(2,1)}, bf16[256,640]{1,0:T(8,128)(2,1)}) custom-call(s32[32]{0:T(128)} %len_ref.1, s32[1]{0:T(128)S(6)} %copy.17.prompt_ref, bf16[256,640]{1,0:T(8,128)(2,1)} %hid_h.1, bf16[256,640]{1,0:T(8,128)(2,1)} %q_h.1, bf16[256,640]{1,0:T(8,128)(2,1)} %kn_h.1, bf16[256,640]{1,0:T(8,128)(2,1)} %vn_h.1, ...), custom_call_target="tpu_custom_call" | custom-call | tf_op jit(solution)/shard_map/pallas_call | solution.py:407
  74.3 1.7 %copy.18 = bf16[256,640]{1,0:T(8,128)(2,1)} copy(bf16[256,640]{1,0:T(8,128)(2,1)} %get-tuple-element.4) | data formatting | bytes 655360
  76.1 1.7 %copy.19 = bf16[256,640]{1,0:T(8,128)(2,1)} copy(bf16[256,640]{1,0:T(8,128)(2,1)} %get-tuple-element.5) | data formatting | bytes 655360

commit v2 on v1

--- a/solution.py
+++ b/solution.py
@@ -12,7 +12,9 @@
 W = NH * HD
 CAP = 4096
 KEYS = CAP + ROWS
-CHUNK = 512
+CHUNK = 1024
+TILES = CHUNK // HD
+TURN = 160
 NEG = -1e30
 SCALE = HD**-0.5
 LOG2E = 1.4426950408889634
@@ -23,9 +25,9 @@
 
 def kernel(
     len_ref, prompt_ref, hid_h, q_h, kn_h, vn_h, ck_h, cv_h, w_h, qc_h, tk_h, tv_h,
-    out_h, cross_h,
-    q_s, kn_s, vn_s, hid_s, qc_s, k_s, v_s, wloc, wall, tk, tv, sbuf, bias, caus,
-    mrun, mfin, lrun, acc, heads, rs_in, rs_out, outb, crossb,
+    outb, crossb,
+    q_s, kn_s, vn_s, hid_s, qc_s, k_s, v_s, wall, tk, tv, sbuf, bias, caus,
+    mrun, mfin, lrun, acc, heads, outt, rs_in, rs_out,
     lsem, kvsem, grecv, gsib, gsend, rrecv, rsend,
 ):
     me = lax.axis_index("req")
@@ -45,7 +47,8 @@
             return (rid(x + by, y, c), z)
         return (rid(x, y + by, c), z)
 
-    wcopy = pltpu.make_async_copy(w_h, wloc, lsem.at[0])
+    mine = pl.multiple_of(me * 160, 32)
+    wcopy = pltpu.make_async_copy(w_h, wall.at[pl.ds(mine, 160)], lsem.at[0])
     wcopy.start()
     small = [
         pltpu.make_async_copy(src, dst, lsem.at[i])
@@ -78,18 +81,6 @@
     for nb in nbrs:
         pl.semaphore_signal(barrier, inc=1, device_id=nb, device_id_type=MESH)
 
-    wcopy.wait()
-    mine = pl.multiple_of(me * 160, 32)
-    wall[pl.ds(mine, 128), :] = wloc[:, 0:128].T
-    wall[pl.ds(pl.multiple_of(mine + 128, 32), 32), :] = wloc[:, 128:160].T
-
-    length = len_ref[me]
-    col = lax.broadcasted_iota(jnp.int32, (8, CAP), 1)
-    bias[...] = jnp.where(col < length, 0.0, NEG).astype(F32)
-    ri = lax.broadcasted_iota(jnp.int32, (ROWS, ROWS), 0)
-    ci = lax.broadcasted_iota(jnp.int32, (ROWS, ROWS), 1)
-    caus[...] = jnp.where(ci <= ri, 0.0, NEG).astype(F32)
-
     def piece(p, ab, ax, ay, ac):
         r = rid(ax, ay, ac)
         if p == 0:
@@ -170,6 +161,7 @@
                 g.wait(1, 0)
                 g.wait(3, 0)
                 g.to_f(-d, 0, d, 2)
+            for g in gs:
                 g.both_g(1)
                 g.both_g(3)
             for g in gs:
@@ -180,13 +172,7 @@
                 g.wait(2, 0)
                 g.both_g(2)
             for g in gs:
-                g.wait(0, 1)
-                g.wait(0, 3)
-                g.to_g(0, -d, d, 0, 2)
-            for g in gs:
                 g.to_sib(2, 0)
-                g.to_sib(0, 1)
-                g.to_sib(0, 3)
         elif n == 3:
             for g in gs:
                 for rf in (1, 3):
@@ -202,12 +188,17 @@
                 g.wait(2, 1)
                 g.wait(2, 3)
                 g.to_g(2, -d, d, 2, 2)
-                g.wait(0, 2)
             for g in gs:
                 g.to_sib(2, 1)
                 g.to_sib(2, 3)
-                g.to_sib(0, 2)
         elif n == 5:
+            for g in gs:
+                g.wait(0, 1)
+                g.wait(0, 3)
+                g.to_g(0, -d, d, 0, 2)
+            for g in gs:
+                g.to_sib(0, 1)
+                g.to_sib(0, 3)
             for g in gs:
                 for rf in (1, 3):
                     g.wait(rf, 2)
@@ -215,7 +206,10 @@
         elif n == 6:
             for g in gs:
                 g.wait(2, 2)
+                g.wait(0, 2)
+            for g in gs:
                 g.to_sib(2, 2)
+                g.to_sib(0, 2)
         else:
             for g in gs:
                 g.wait_sib()
@@ -233,8 +227,10 @@
         s = lax.dot_general(q_s[:, sl], k_s[h, pl.ds(at, CHUNK), :], NT, preferred_element_type=F32)
         s = s + bias[0:1, pl.ds(at, CHUNK)]
         sbuf[h % 2, :, pl.ds(at, CHUNK)] = s
-        m = jnp.maximum(jnp.maximum(s[:, 0:128], s[:, 128:256]), jnp.maximum(s[:, 256:384], s[:, 384:512]))
-        mrun[...] = jnp.maximum(mrun[...], m)
+        m = mrun[...]
+        for t in range(TILES):
+            m = jnp.maximum(m, s[:, t * HD:(t + 1) * HD])
+        mrun[...] = m
 
     def set_max():
         mfin[...] = jnp.broadcast_to(jnp.max(mrun[...], axis=1, keepdims=True), (ROWS, HD))
@@ -260,8 +256,8 @@
 
     def pv_chunk(h, i):
         at = pl.multiple_of(i * CHUNK, CHUNK)
-        p = weigh(sbuf[h % 2, :, pl.ds(at, CHUNK)], 4)
-        part, o = pv(p, v_s[h, pl.ds(at, CHUNK), :], 4)
+        p = weigh(sbuf[h % 2, :, pl.ds(at, CHUNK)], TILES)
+        part, o = pv(p, v_s[h, pl.ds(at, CHUNK), :], TILES)
         lrun[...] += part
         acc[...] += o
 
@@ -300,48 +296,67 @@
         o = jnp.dot(p.astype(BF16), vt, preferred_element_type=F32)
         crossb[:, sl] = (o / mass).astype(BF16)
 
-    groups = ((0, 3), (3, 2))
-
-    def term(g, s):
-        first, count = groups[g]
-        way = d if g == 0 else -d
-        b = (z - way * (1 + s) + 16) % 8
-        at = pl.multiple_of(b * W + first * HD, HD)
-        wt = wall[pl.ds(at, count * HD), :]
-        return lax.dot_general(heads[...], wt, NT, preferred_element_type=F32)
-
-    def rs_copy(g, j, s):
-        way = d if g == 0 else -d
+    flows = ((d, 4), (-d, 3))
+    PARTS = W // TURN
+
+    def term(b, k):
+        at = pl.multiple_of(b * W + k * TURN, 32)
+        return lax.dot_general(wall[pl.ds(at, TURN), :], heads[...], NT, preferred_element_type=F32)
+
+    def rs_copy(f, s, k):
+        way = flows[f][0]
         return pltpu.make_async_remote_copy(
-            src_ref=rs_out.at[j, s], dst_ref=rs_in.at[j, s],
-            send_sem=rsend.at[j, s], recv_sem=rrecv.at[j, s],
+            src_ref=rs_out.at[f, s, k], dst_ref=rs_in.at[f, s, k],
+            send_sem=rsend.at[f, s, k], recv_sem=rrecv.at[f, s, k],
             device_id=(me, (z + way + 8) % 8), device_id_type=MESH,
         )
 
+    def rs_block(f, s):
+        way, hops = flows[f]
+        return (z + (hops - s) * way + 8) % 8
+
     def rs_first():
-        for g, (first, count) in enumerate(groups):
-            t = term(g, 0)
-            for k in range(count):
-                rs_out[first + k, 0] = t[:, k * HD:(k + 1) * HD].astype(BF16)
-            for k in range(count):
-                rs_copy(g, first + k, 0).start()
+        for k in range(PARTS):
+            for f in range(2):
+                rs_out[f, 0, k] = term(rs_block(f, 0), k).astype(BF16)
+                rs_copy(f, 0, k).start()
 
     def rs_step(s):
-        for g, (first, count) in enumerate(groups):
-            t = term(g, s + 1)
-            for k in range(count):
-                j = first + k
-                rs_copy(g, j, s).wait_recv()
-                total = rs_in[j, s].astype(F32) + t[:, k * HD:(k + 1) * HD]
-                if s < 6:
-                    rs_out[j, s + 1] = total.astype(BF16)
-                    rs_copy(g, j, s + 1).start()
-                else:
-                    sl = slice(j * HD, (j + 1) * HD)
-                    outb[:, sl] = (hid_s[:, sl].astype(F32) + total).astype(BF16)
-
+        for k in range(PARTS):
+            for f in range(2):
+                if s < flows[f][1]:
+                    t = term(rs_block(f, s), k)
+                    rs_copy(f, s - 1, k).wait_recv()
+                    rs_out[f, s, k] = (rs_in[f, s - 1, k].astype(F32) + t).astype(BF16)
+                    rs_copy(f, s, k).start()
+
+    def rs_own():
+        for k in range(PARTS):
+            t = term(z, k)
+            rs_copy(1, 2, k).wait_recv()
+            outt[k * TURN:(k + 1) * TURN, :] = t + rs_in[1, 2, k].astype(F32)
+
+    def rs_last():
+        for k in range(PARTS):
+            rs_copy(0, 3, k).wait_recv()
+            at = slice(k * TURN, (k + 1) * TURN)
+            outt[at, :] = outt[at, :] + rs_in[0, 3, k].astype(F32)
+        for j in range(NH):
+            sl = slice(j * HD, (j + 1) * HD)
+            outb[:, sl] = (hid_s[:, sl].astype(F32) + outt[sl, :].T).astype(BF16)
+
+    def masks():
+        length = len_ref[me]
+        col = lax.broadcasted_iota(jnp.int32, (8, CAP), 1)
+        bias[...] = jnp.where(col < length, 0.0, NEG).astype(F32)
+        ri = lax.broadcasted_iota(jnp.int32, (ROWS, ROWS), 0)
+        ci = lax.broadcasted_iota(jnp.int32, (ROWS, ROWS), 1)
+        caus[...] = jnp.where(ci <= ri, 0.0, NEG).astype(F32)
+
+    wcopy.wait()
     pl.semaphore_wait(barrier, len(nbrs))
     stage(0, 0)
+    masks()
     for cp in small[:3]:
         cp.wait()
     head_stage(0)
@@ -353,48 +368,37 @@
     head_stage(4)
     stage(0, 3)
     head_stage(5)
+    stage(0, 4)
     for cp in own_text:
         cp.wait()
-    stage(0, 4)
+    stage(0, 5)
     stage(1, 0)
-    stage(0, 5)
     stage(0, 6)
     stage(0, 7)
     rs_first()
     for cp in small[3:]:
         cp.wait()
-    rs_step(0)
     stage(1, 1)
     rs_step(1)
     stage(1, 2)
+    stage(1, 3)
     rs_step(2)
-    stage(1, 3)
-    rs_step(3)
     stage(1, 4)
-    rs_step(4)
     stage(1, 5)
     stage(1, 6)
+    rs_step(3)
     stage(1, 7)
-    cross_head(0)
-    cross_head(1)
-    cross_head(2)
-    rs_step(5)
-    cross_head(3)
-    cross_head(4)
-    cross_out = pltpu.make_async_copy(crossb, cross_h, lsem.at[8])
-    cross_out.start()
-    rs_step(6)
-    hid_out = pltpu.make_async_copy(outb, out_h, lsem.at[9])
-    hid_out.start()
+    rs_own()
+    for h in range(NH):
+        cross_head(h)
+    rs_last()
     for ps in pairs:
         for g in ps:
             g.wait_send()
-    for g, (first, count) in enumerate(groups):
-        for k in range(count):
-            for s in range(7):
-                rs_copy(g, first + k, s).wait_send()
-    cross_out.wait()
-    hid_out.wait()
+    for k in range(PARTS):
+        for f in range(2):
+            for s in range(flows[f][1]):
+                rs_copy(f, s, k).wait_send()
 
 
 def per_device(
@@ -404,30 +408,27 @@
     smem = pl.BlockSpec(memory_space=pltpu.SMEM)
     v = pltpu.VMEM
     dma = pltpu.SemaphoreType.DMA
+    vmem = pl.BlockSpec(memory_space=pltpu.VMEM)
     return pl.pallas_call(
         kernel,
-        out_shape=(
-            jax.ShapeDtypeStruct((ROWS, W), BF16),
-            jax.ShapeDtypeStruct((ROWS, W), BF16),
-        ),
+        out_shape=(v((ROWS, W), BF16), v((ROWS, W), BF16)),
         in_specs=[smem, smem] + [any_spec] * 10,
-        out_specs=(any_spec, any_spec),
+        out_specs=(vmem, vmem),
         scratch_shapes=[
             v((ROWS, W), BF16), v((ROWS, W), BF16), v((ROWS, W), BF16), v((ROWS, W), BF16), v((ROWS, W), BF16),
             v((NH, CAP, HD), BF16), v((NH, CAP, HD), BF16),
-            v((W, 160), BF16), v((8 * W, W), BF16),
+            v((8 * W, W), BF16),
             v((32, 4, 16, W), BF16), v((32, 4, 16, W), BF16),
             v((2, ROWS, KEYS), F32), v((8, CAP), F32), v((ROWS, ROWS), F32),
             v((ROWS, HD), F32), v((ROWS, HD), F32), v((ROWS, HD), F32), v((ROWS, HD), F32),
-            v((ROWS, W), BF16),
-            v((NH, 7, ROWS, HD), BF16), v((NH, 7, ROWS, HD), BF16),
-            v((ROWS, W), BF16), v((ROWS, W), BF16),
-            dma((10,)), dma((2, NH)), dma((2, 2, 16)), dma((2, 2)), dma((2, 2)), dma((NH, 7)), dma((NH, 7)),
+            v((ROWS, W), BF16), v((W, ROWS), F32),
+            v((2, 4, 4, TURN, ROWS), BF16), v((2, 4, 4, TURN, ROWS), BF16),
+            dma((8,)), dma((2, NH)), dma((2, 2, 16)), dma((2, 2)), dma((2, 2)), dma((2, 4, 4)), dma((2, 4, 4)),
         ],
         compiler_params=pltpu.CompilerParams(
-            collective_id=0, has_side_effects=True, vmem_limit_bytes=60 * 1024 * 1024
+            collective_id=0, has_side_effects=True, vmem_limit_bytes=56 * 1024 * 1024
         ),
-    )(cache_len, prompt_of, hidden, q_new, k_new, v_new, cache_k, cache_v, w_out, q_cross, text_k, text_v)
+    )(cache_len, prompt_of, hidden, q_new, k_new, v_new, cache_k, cache_v, w_out.T, q_cross, text_k, text_v)
 
 
 def solution(mesh):

time: 78 us -> 64.6 us (0.83)
  Pallas kernels: 71.2 us -> 61.8 us
  local copies, waits for them, and re-layouts: 5.28 us -> 1.45 us
    pallas_call x1, Pallas kernels: 71.2 us -> 61.8 us  [per_device(): pl.pallas_call(kernel, out_shape=(v((ROWS, W), BF16), v((ROWS, W), BF16))...]
    unnamed x3 -> x2, local copies, waits for them, and re-layouts: 5.28 us -> 1.45 us
where the time goes in v2:
time: 64.6 us; the launch traced here: 64.5 us
  Pallas kernels  61.8 us (96%)
  local copies, waits for them, and re-layouts  1.45 us (2%)
  between operations  1.29 us (2%)
    pallas_call x1, Pallas kernels, per_device(): pl.pallas_call(kernel, out_shape=(v((ROWS, W), BF16), v((ROWS, W), BF16))...  61.8 us
    unnamed x2, local copies, waits for them, and re-layouts  1.45 us

profile of v2, /device:TPU:1, one launch (start us, length us, event | category | flops | bytes accessed | tf_op | source)
XLA Modules:
  0.0 64.5 jit_solution(9616919776987626682)
XLA Ops:
  1.3 61.8 %shard_map.131 = (bf16[256,640]{1,0:T(8,128)(2,1)S(1)}, bf16[256,640]{1,0:T(8,128)(2,1)S(1)}) custom-call(s32[32]{0:T(128)} %len_ref.1, s32[1]{0:T(128)S(6)} %copy.18.prompt_ref, bf16[256,640]{1,0:T(8,128)(2,1)} %hid_h.1, bf16[256,640]{1,0:T(8,128)(2,1)} %q_h.1, bf16[256,640]{1,0:T(8,128)(2,1)} %kn_h.1, bf16[256,640]{1,0:T(8,128)(2,1)} %vn_h.1, ...), custom_call_target="tpu_custom_call" | custom-call | tf_op jit(solution)/shard_map/pallas_call | solution.py:412
  63.1 0.7 %copy.16 = bf16[256,640]{1,0:T(8,128)(2,1)} copy(bf16[256,640]{1,0:T(8,128)(2,1)S(1)} %get-tuple-element.2) | data formatting | bytes 655360
  63.8 0.7 %copy.17 = bf16[256,640]{1,0:T(8,128)(2,1)} copy(bf16[256,640]{1,0:T(8,128)(2,1)S(1)} %get-tuple-element.3) | data formatting | bytes 655360

commit v3 on v2

--- a/solution.py
+++ b/solution.py
@@ -14,7 +14,8 @@
 KEYS = CAP + ROWS
 CHUNK = 1024
 TILES = CHUNK // HD
-TURN = 160
+HALVES = (48, 32)
+PART = 128
 NEG = -1e30
 SCALE = HD**-0.5
 LOG2E = 1.4426950408889634
@@ -26,7 +27,7 @@
 def kernel(
     len_ref, prompt_ref, hid_h, q_h, kn_h, vn_h, ck_h, cv_h, w_h, qc_h, tk_h, tv_h,
     outb, crossb,
-    q_s, kn_s, vn_s, hid_s, qc_s, k_s, v_s, wall, tk, tv, sbuf, bias, caus,
+    q_s, kn_s, vn_s, hid_s, qc_s, k_s, v_s, wall0, wall1, tk, tv, sbuf, bias, caus,
     mrun, mfin, lrun, acc, heads, outt, rs_in, rs_out,
     lsem, kvsem, grecv, gsib, gsend, rrecv, rsend,
 ):
@@ -47,9 +48,18 @@
             return (rid(x + by, y, c), z)
         return (rid(x, y + by, c), z)
 
-    mine = pl.multiple_of(me * 160, 32)
-    wcopy = pltpu.make_async_copy(w_h, wall.at[pl.ds(mine, 160)], lsem.at[0])
-    wcopy.start()
+    walls = (wall0, wall1)
+
+    def own_rows(p):
+        n = 2 * HALVES[p]
+        return walls[p].at[pl.ds(pl.multiple_of(me * n, n), n)]
+
+    wcopies = (
+        pltpu.make_async_copy(w_h.at[pl.ds(0, 96)], own_rows(0), lsem.at[0]),
+        pltpu.make_async_copy(w_h.at[pl.ds(96, 64)], own_rows(1), lsem.at[8]),
+    )
+    for cp in wcopies:
+        cp.start()
     small = [
         pltpu.make_async_copy(src, dst, lsem.at[i])
         for i, (src, dst) in enumerate([(q_h, q_s), (kn_h, kn_s), (vn_h, vn_s), (hid_h, hid_s), (qc_h, qc_s)], 1)
@@ -83,13 +93,14 @@
 
     def piece(p, ab, ax, ay, ac):
         r = rid(ax, ay, ac)
-        if p == 0:
-            return wall.at[pl.ds(pl.multiple_of(r * 160 + ab * 80, 16), 80)]
+        if p < 2:
+            n = HALVES[p]
+            return walls[p].at[pl.ds(pl.multiple_of(r * 2 * n + ab * n, n), n)]
         return (tk if ab == 0 else tv).at[r]
 
     def some(p, ab, n):
-        if p == 0:
-            return wall.at[pl.ds(0, 80 * n)]
+        if p < 2:
+            return walls[p].at[pl.ds(0, HALVES[p] * n)]
         return (tk if ab == 0 else tv).at[pl.ds(0, n)]
 
     class Gather:
@@ -144,7 +155,7 @@
         def wait_send(self):
             self.copy(some(self.p, self.ab, 31), sib, 0, 0).wait_send()
 
-    pairs = [(Gather(0, 0), Gather(0, 1)), (Gather(1, 0), Gather(1, 1))]
+    pairs = [(Gather(p, 0), Gather(p, 1)) for p in range(3)]
 
     def stage(p, n):
         gs = pairs[p]
@@ -297,11 +308,15 @@
         crossb[:, sl] = (o / mass).astype(BF16)
 
     flows = ((d, 4), (-d, 3))
-    PARTS = W // TURN
-
-    def term(b, k):
-        at = pl.multiple_of(b * W + k * TURN, 32)
-        return lax.dot_general(wall[pl.ds(at, TURN), :], heads[...], NT, preferred_element_type=F32)
+    parts = ((0, 1, 2), (3, 4))
+
+    def term(b, p):
+        n = 8 * HALVES[p]
+        wt = walls[p][pl.ds(pl.multiple_of(b * n, n), n), :]
+        return lax.dot_general(wt, heads[...], NT, preferred_element_type=F32)
+
+    def cut(t, i):
+        return t[i * PART:(i + 1) * PART]
 
     def rs_copy(f, s, k):
         way = flows[f][0]
@@ -315,32 +330,45 @@
         way, hops = flows[f]
         return (z + (hops - s) * way + 8) % 8
 
-    def rs_first():
-        for k in range(PARTS):
-            for f in range(2):
-                rs_out[f, 0, k] = term(rs_block(f, 0), k).astype(BF16)
+    def rs_first(p):
+        for f in range(2):
+            t = term(rs_block(f, 0), p)
+            for i, k in enumerate(parts[p]):
+                rs_out[f, 0, k] = cut(t, i).astype(BF16)
                 rs_copy(f, 0, k).start()
 
-    def rs_step(s):
-        for k in range(PARTS):
-            for f in range(2):
-                if s < flows[f][1]:
-                    t = term(rs_block(f, s), k)
-                    rs_copy(f, s - 1, k).wait_recv()
-                    rs_out[f, s, k] = (rs_in[f, s - 1, k].astype(F32) + t).astype(BF16)
-                    rs_copy(f, s, k).start()
-
-    def rs_own():
-        for k in range(PARTS):
-            t = term(z, k)
+    def rs_step(s, p):
+        live = [f for f in range(2) if s < flows[f][1]]
+        terms = {f: term(rs_block(f, s), p) for f in live}
+        for i, k in enumerate(parts[p]):
+            for f in live:
+                rs_copy(f, s - 1, k).wait_recv()
+                rs_out[f, s, k] = (rs_in[f, s - 1, k].astype(F32) + cut(terms[f], i)).astype(BF16)
+                rs_copy(f, s, k).start()
+
+    def spans(p, i):
+        n = 2 * HALVES[p]
+        lo, end = i * PART, (i + 1) * PART
+        while lo < end:
+            hi = min(end, (lo // n + 1) * n)
+            to = lo // n * 160 + lo % n + (96 if p else 0)
+            yield slice(lo - i * PART, hi - i * PART), slice(to, to + hi - lo)
+            lo = hi
+
+    def rs_own(p):
+        t = term(z, p)
+        for i, k in enumerate(parts[p]):
             rs_copy(1, 2, k).wait_recv()
-            outt[k * TURN:(k + 1) * TURN, :] = t + rs_in[1, 2, k].astype(F32)
+            total = cut(t, i) + rs_in[1, 2, k].astype(F32)
+            for src, dst in spans(p, i):
+                outt[dst, :] = total[src]
 
     def rs_last():
-        for k in range(PARTS):
-            rs_copy(0, 3, k).wait_recv()
-            at = slice(k * TURN, (k + 1) * TURN)
-            outt[at, :] = outt[at, :] + rs_in[0, 3, k].astype(F32)
+        for p in range(2):
+            for i, k in enumerate(parts[p]):
+                rs_copy(0, 3, k).wait_recv()
+                for src, dst in spans(p, i):
+                    outt[dst, :] = outt[dst, :] + rs_in[0, 3, k, src].astype(F32)
         for j in range(NH):
             sl = slice(j * HD, (j + 1) * HD)
             outb[:, sl] = (hid_s[:, sl].astype(F32) + outt[sl, :].T).astype(BF16)
@@ -353,9 +381,11 @@
         ci = lax.broadcasted_iota(jnp.int32, (ROWS, ROWS), 1)
         caus[...] = jnp.where(ci <= ri, 0.0, NEG).astype(F32)
 
-    wcopy.wait()
+    for cp in wcopies:
+        cp.wait()
     pl.semaphore_wait(barrier, len(nbrs))
     stage(0, 0)
+    stage(1, 0)
     masks()
     for cp in small[:3]:
         cp.wait()
@@ -363,42 +393,55 @@
     head_stage(1)
     stage(0, 1)
     head_stage(2)
+    stage(0, 2)
+    stage(1, 1)
+    stage(0, 3)
     head_stage(3)
-    stage(0, 2)
+    stage(0, 4)
+    stage(1, 2)
     head_stage(4)
-    stage(0, 3)
+    stage(0, 5)
+    stage(0, 6)
+    stage(1, 3)
     head_stage(5)
-    stage(0, 4)
+    stage(0, 7)
+    rs_first(0)
+    stage(1, 4)
     for cp in own_text:
         cp.wait()
-    stage(0, 5)
-    stage(1, 0)
-    stage(0, 6)
-    stage(0, 7)
-    rs_first()
+    stage(1, 5)
+    stage(2, 0)
+    stage(1, 6)
+    stage(1, 7)
+    rs_first(1)
     for cp in small[3:]:
         cp.wait()
-    stage(1, 1)
-    rs_step(1)
-    stage(1, 2)
-    stage(1, 3)
-    rs_step(2)
-    stage(1, 4)
-    stage(1, 5)
-    stage(1, 6)
-    rs_step(3)
-    stage(1, 7)
-    rs_own()
+    rs_step(1, 0)
+    stage(2, 1)
+    rs_step(1, 1)
+    stage(2, 2)
+    rs_step(2, 0)
+    stage(2, 3)
+    rs_step(2, 1)
+    stage(2, 4)
+    stage(2, 5)
+    stage(2, 6)
+    rs_step(3, 0)
+    rs_own(0)
+    rs_step(3, 1)
+    stage(2, 7)
+    rs_own(1)
     for h in range(NH):
         cross_head(h)
     rs_last()
     for ps in pairs:
         for g in ps:
             g.wait_send()
-    for k in range(PARTS):
-        for f in range(2):
-            for s in range(flows[f][1]):
-                rs_copy(f, s, k).wait_send()
+    for p in range(2):
+        for k in parts[p]:
+            for f in range(2):
+                for s in range(flows[f][1]):
+                    rs_copy(f, s, k).wait_send()
 
 
 def per_device(
@@ -417,13 +460,13 @@
         scratch_shapes=[
             v((ROWS, W), BF16), v((ROWS, W), BF16), v((ROWS, W), BF16), v((ROWS, W), BF16), v((ROWS, W), BF16),
             v((NH, CAP, HD), BF16), v((NH, CAP, HD), BF16),
-            v((8 * W, W), BF16),
+            v((64 * HALVES[0], W), BF16), v((64 * HALVES[1], W), BF16),
             v((32, 4, 16, W), BF16), v((32, 4, 16, W), BF16),
             v((2, ROWS, KEYS), F32), v((8, CAP), F32), v((ROWS, ROWS), F32),
             v((ROWS, HD), F32), v((ROWS, HD), F32), v((ROWS, HD), F32), v((ROWS, HD), F32),
             v((ROWS, W), BF16), v((W, ROWS), F32),
-            v((2, 4, 4, TURN, ROWS), BF16), v((2, 4, 4, TURN, ROWS), BF16),
-            dma((8,)), dma((2, NH)), dma((2, 2, 16)), dma((2, 2)), dma((2, 2)), dma((2, 4, 4)), dma((2, 4, 4)),
+            v((2, 4, NH, PART, ROWS), BF16), v((2, 4, NH, PART, ROWS), BF16),
+            dma((9,)), dma((2, NH)), dma((3, 2, 16)), dma((3, 2)), dma((3, 2)), dma((2, 4, NH)), dma((2, 4, NH)),
         ],
         compiler_params=pltpu.CompilerParams(
             collective_id=0, has_side_effects=True, vmem_limit_bytes=56 * 1024 * 1024

time: 64.6 us -> 65.5 us (1.014)
  Pallas kernels: 61.8 us -> 62.6 us
    pallas_call x1, Pallas kernels: 61.8 us -> 62.6 us  [per_device(): pl.pallas_call(kernel, out_shape=(v((ROWS, W), BF16), v((ROWS, W), BF16))...]
where the time goes in v3:
time: 65.5 us; the launch traced here: 65.4 us
  Pallas kernels  62.6 us (96%)
  local copies, waits for them, and re-layouts  1.45 us (2%)
  between operations  1.29 us (2%)
    pallas_call x1, Pallas kernels, per_device(): pl.pallas_call(kernel, out_shape=(v((ROWS, W), BF16), v((ROWS, W), BF16))...  62.6 us
    unnamed x2, local copies, waits for them, and re-layouts  1.45 us

profile of v3, /device:TPU:1, one launch (start us, length us, event | category | flops | bytes accessed | tf_op | source)
XLA Modules:
  0.0 65.4 jit_solution(4325162798416430675)
XLA Ops:
  1.3 62.6 %shard_map.131 = (bf16[256,640]{1,0:T(8,128)(2,1)S(1)}, bf16[256,640]{1,0:T(8,128)(2,1)S(1)}) custom-call(s32[32]{0:T(128)} %len_ref.1, s32[1]{0:T(128)S(6)} %copy.18.prompt_ref, bf16[256,640]{1,0:T(8,128)(2,1)} %hid_h.1, bf16[256,640]{1,0:T(8,128)(2,1)} %q_h.1, bf16[256,640]{1,0:T(8,128)(2,1)} %kn_h.1, bf16[256,640]{1,0:T(8,128)(2,1)} %vn_h.1, ...), custom_call_target="tpu_custom_call" | custom-call | tf_op jit(solution)/shard_map/pallas_call | solution.py:455
  63.9 0.7 %copy.16 = bf16[256,640]{1,0:T(8,128)(2,1)} copy(bf16[256,640]{1,0:T(8,128)(2,1)S(1)} %get-tuple-element.2) | data formatting | bytes 655360
  64.7 0.7 %copy.17 = bf16[256,640]{1,0:T(8,128)(2,1)} copy(bf16[256,640]{1,0:T(8,128)(2,1)S(1)} %get-tuple-element.3) | data formatting | bytes 655360

commit v4 on v2

--- a/solution.py
+++ b/solution.py
@@ -189,16 +189,14 @@
                 g.wait(2, 3)
                 g.to_g(2, -d, d, 2, 2)
             for g in gs:
-                g.to_sib(2, 1)
-                g.to_sib(2, 3)
-        elif n == 5:
-            for g in gs:
                 g.wait(0, 1)
                 g.wait(0, 3)
                 g.to_g(0, -d, d, 0, 2)
             for g in gs:
-                g.to_sib(0, 1)
-                g.to_sib(0, 3)
+                for rg in (1, 3):
+                    g.to_sib(2, rg)
+                    g.to_sib(0, rg)
+        elif n == 5:
             for g in gs:
                 for rf in (1, 3):
                     g.wait(rf, 2)
@@ -337,13 +335,16 @@
             outt[k * TURN:(k + 1) * TURN, :] = t + rs_in[1, 2, k].astype(F32)
 
     def rs_last():
+        done = 0
         for k in range(PARTS):
             rs_copy(0, 3, k).wait_recv()
             at = slice(k * TURN, (k + 1) * TURN)
             outt[at, :] = outt[at, :] + rs_in[0, 3, k].astype(F32)
-        for j in range(NH):
-            sl = slice(j * HD, (j + 1) * HD)
-            outb[:, sl] = (hid_s[:, sl].astype(F32) + outt[sl, :].T).astype(BF16)
+            ready = (k + 1) * TURN // HD
+            for j in range(done, ready):
+                sl = slice(j * HD, (j + 1) * HD)
+                outb[:, sl] = (hid_s[:, sl].astype(F32) + outt[sl, :].T).astype(BF16)
+            done = ready
 
     def masks():
         length = len_ref[me]
@@ -371,8 +372,8 @@
     stage(0, 4)
     for cp in own_text:
         cp.wait()
+    stage(1, 0)
     stage(0, 5)
-    stage(1, 0)
     stage(0, 6)
     stage(0, 7)
     rs_first()

time: 64.6 us -> 65.8 us (1.019)
  Pallas kernels: 61.8 us -> 62.9 us
    pallas_call x1, Pallas kernels: 61.8 us -> 62.9 us  [per_device(): pl.pallas_call(kernel, out_shape=(v((ROWS, W), BF16), v((ROWS, W), BF16))...]
where the time goes in v4:
time: 65.8 us; the launch traced here: 65.7 us
  Pallas kernels  62.9 us (96%)
  local copies, waits for them, and re-layouts  1.45 us (2%)
  between operations  1.29 us (2%)
    pallas_call x1, Pallas kernels, per_device(): pl.pallas_call(kernel, out_shape=(v((ROWS, W), BF16), v((ROWS, W), BF16))...  62.9 us
    unnamed x2, local copies, waits for them, and re-layouts  1.45 us

profile of v4, /device:TPU:1, one launch (start us, length us, event | category | flops | bytes accessed | tf_op | source)
XLA Modules:
  0.0 65.7 jit_solution(18261152633035555524)
XLA Ops:
  1.3 62.9 %shard_map.131 = (bf16[256,640]{1,0:T(8,128)(2,1)S(1)}, bf16[256,640]{1,0:T(8,128)(2,1)S(1)}) custom-call(s32[32]{0:T(128)} %len_ref.1, s32[1]{0:T(128)S(6)} %copy.18.prompt_ref, bf16[256,640]{1,0:T(8,128)(2,1)} %hid_h.1, bf16[256,640]{1,0:T(8,128)(2,1)} %q_h.1, bf16[256,640]{1,0:T(8,128)(2,1)} %kn_h.1, bf16[256,640]{1,0:T(8,128)(2,1)} %vn_h.1, ...), custom_call_target="tpu_custom_call" | custom-call | tf_op jit(solution)/shard_map/pallas_call | solution.py:413
  64.2 0.7 %copy.16 = bf16[256,640]{1,0:T(8,128)(2,1)} copy(bf16[256,640]{1,0:T(8,128)(2,1)S(1)} %get-tuple-element.2) | data formatting | bytes 655360
  65.0 0.7 %copy.17 = bf16[256,640]{1,0:T(8,128)(2,1)} copy(bf16[256,640]{1,0:T(8,128)(2,1)S(1)} %get-tuple-element.3) | data formatting | bytes 655360
